TPU v7x, 32 devices: a whole 2x2x4 slice. The times are simulated.
32 devices in a mesh: groups: 2 (over x), tile: 16 (over z, y, core).
Axes of the slice: x: 2, y: 2, z: 4, core: 2. Of those that a mesh axis runs over, the one named last changes fastest.
Arguments:
- hidden: bfloat16 [12288, 1152], P(('groups', 'tile')), parts along dimension 0, may hold values from -40 to 40
- keep_mask: int32 [12288], P(('groups', 'tile')), parts along dimension 0, may hold values 0 or 1
- kept_embed: bfloat16 [1152], replicated, may hold values from -6 to 6
- time_mod: bfloat16 [50, 6, 1152], replicated, may hold values from -3 to 3
- timestep: int32 [2], P('groups'), parts along dimension 0, may hold values from 0 to 49
- qkv_weight: bfloat16 [1152, 3456], replicated, may hold values from -0.1875 to 0.1875
- proj_weight: bfloat16 [1152, 1152], replicated, may hold values from -0.1875 to 0.1875
- norm_gain: bfloat16 [1152], replicated, may hold values from 0.099609375 to 1.8984375
- in_weight: bfloat16 [1152, 5760], P('tile'), may hold values from -0.1875 to 0.1875
- in_bias: bfloat16 [5760], replicated, may hold values from -3 to 3
- conv_weight: bfloat16 [3, 3, 5760], replicated, may hold values from -2 to 2
- conv_bias: bfloat16 [5760], replicated, may hold values from -3 to 3
- out_weight: bfloat16 [2880, 1152], P(None, 'tile'), may hold values from -0.109375 to 0.109375
Outputs:
- output: bfloat16 [12288, 1152], P(('groups', 'tile')), parts along dimension 0
There are 2 independent parts, one for each index of `groups`. A program takes and returns all parts, laid end to end along the dimension named above; an argument that names none is the same for every part. Nothing has to cross between parts.
All inputs are finite; a program needn't handle non-finite values. No bound on the sum of `keep_mask` on one device may be relied on, other than what follows from the above.
Results may differ from a plain program's by a relative error of at most 0.0015.
The roundings to bfloat16 on the way count: a program that leaves them out, or rounds other values in their place, can miss the bound.
Values may be sent and summed in bfloat16 or wider, within the bound.
A program may use at most 192 MiB of HBM per device.

v0:
```python
import jax
import jax.numpy as jnp
from jax import lax
from jax.sharding import PartitionSpec as P

D = 1152
HEADS = 36
HEAD_DIM = 32
FF = 2880
CANVAS_W = 128


def padded_2(cells, sides, width):
    for axis, dim in sides:
        count = lax.axis_size(axis)
        ends = count - 1
        head = lax.slice_in_dim(cells, 0, width, axis=dim)
        tail = lax.slice_in_dim(cells, cells.shape[dim] - width, cells.shape[dim], axis=dim)
        cells = jnp.concatenate(
            [
                lax.ppermute(tail, axis, [(i, (i + 1) % count) for i in range(ends)]),
                cells,
                lax.ppermute(head, axis, [((i + 1) % count, i) for i in range(ends)]),
            ],
            axis=dim,
        )
    return cells


def modulated_norm(stream, shift, scale):
    factor = lax.rsqrt(jnp.mean(stream * stream, axis=-1, keepdims=True) + 1e-06)
    return stream * factor * (1.0 + scale) + shift


def convolve(window, conv_weight, conv_bias, count):
    width = window.shape[1] - 2
    total = jnp.zeros((count, width, window.shape[2]), jnp.float32) + conv_bias.astype(jnp.float32)
    for row_off in range(3):
        for col_off in range(3):
            total = total + window[row_off : row_off + count, col_off : col_off + width, :].astype(
                jnp.float32
            ) * conv_weight[row_off, col_off].astype(jnp.float32)
    return total


def row_folder(source, piece):
    return jnp.dot(source, piece, preferred_element_type=jnp.float32)


def local(
    hidden,
    keep_mask,
    kept_embed,
    time_mod,
    timestep,
    qkv_weight,
    proj_weight,
    norm_gain,
    in_weight,
    in_bias,
    conv_weight,
    conv_bias,
    out_weight,
):
    modulation = lax.dynamic_index_in_dim(time_mod, timestep[0], 0, keepdims=False).astype(
        jnp.float32
    )
    tokens = hidden.shape[0]
    rows = tokens // CANVAS_W
    stream = (
        hidden.astype(jnp.float32)
        + keep_mask.astype(jnp.float32)[:, None] * kept_embed.astype(jnp.float32)[None, :]
    )
    normed_in = modulated_norm(stream, modulation[0], modulation[1]).astype(jnp.bfloat16)
    mixed_qkv = jnp.dot(normed_in, qkv_weight, preferred_element_type=jnp.float32)
    query = jax.nn.relu(mixed_qkv[:, :D]).astype(jnp.bfloat16).reshape(tokens, HEADS, HEAD_DIM)
    key_rows = (
        jax.nn.relu(mixed_qkv[:, D : 2 * D]).astype(jnp.bfloat16).reshape(tokens, HEADS, HEAD_DIM)
    )
    values = mixed_qkv[:, 2 * D :].astype(jnp.bfloat16).reshape(tokens, HEADS, HEAD_DIM)
    local_state = jnp.einsum("thd,the->hde", key_rows, values, preferred_element_type=jnp.float32)
    state = lax.psum(local_state, "tile")
    attended = jnp.einsum(
        "thd,hde->the", query.astype(jnp.float32), state, precision=lax.Precision.HIGHEST
    ).reshape(tokens, D)
    factor = lax.rsqrt(jnp.mean(attended * attended, axis=-1, keepdims=True) + 1e-06)
    normed_attn = (attended * factor * norm_gain.astype(jnp.float32)).astype(jnp.bfloat16)
    after_attn = stream + modulation[2] * jnp.dot(
        normed_attn, proj_weight, preferred_element_type=jnp.float32
    )
    normed_ffn = modulated_norm(after_attn, modulation[3], modulation[4]).astype(jnp.bfloat16)
    before = row_folder(normed_ffn, lax.all_gather(in_weight, "tile", axis=0, tiled=True))
    inner = (
        jax.nn.silu(before + in_bias.astype(jnp.float32))
        .astype(jnp.bfloat16)
        .reshape(rows, CANVAS_W, 2 * FF)
    )
    framed = padded_2(inner, (("tile", 0),), 1)
    padded = jnp.pad(framed, ((0, 0), (1, 1), (0, 0)))
    conv = convolve(padded, conv_weight, conv_bias, rows)
    gated = (conv[..., :FF] * jax.nn.silu(conv[..., FF:])).astype(jnp.bfloat16).reshape(tokens, FF)
    projected = jnp.dot(
        gated,
        lax.all_gather(out_weight, "tile", axis=1, tiled=True),
        preferred_element_type=jnp.float32,
    )
    return (after_attn + modulation[5] * projected).astype(jnp.bfloat16)


def solution(mesh):
    in_specs = (
        P(("groups", "tile"), None),
        P(("groups", "tile")),
        P(),
        P(),
        P("groups"),
        P(),
        P(),
        P(),
        P("tile", None),
        P(),
        P(),
        P(),
        P(None, "tile"),
    )
    out_specs = P(("groups", "tile"), None)
    return jax.shard_map(local, mesh=mesh, in_specs=in_specs, out_specs=out_specs, check_vma=False)
```

profile of v0, /device:TPU:0, one launch (start us, length us, event | category | flops | bytes accessed | tf_op | source)
XLA Modules:
  0.0 325.5 jit_solution(18351720821955758159)
XLA Ops:
  6.5 0.0 copy-start
  6.5 0.0 all-reduce.3.cloned.1.call-start
  7.3 0.9 dynamic-slice_convert_fusion
  8.3 0.7 slice_reduce_fusion.1
  8.9 0.7 convert_element_type.97
  9.6 0.7 convert_element_type.96
  10.3 1.6 multiply_reduce_fusion.1
  11.9 7.5 %fusion.15 = bf16[384,3456]{1,0:T(8,128)(2,1)S(1)} fusion(bf16[1152,3456]{1,0:T(8,128)(2,1)} %param.18, bf16[384,1152]{1,0:T(8,128)(2,1)} %param.13, f32[1152]{0:T(1024)S(1)} %get-tuple-element.17, f32[1152]{0:T(1024)S(1)} %get-tuple-element.18, f32[384]{0:T(512)S(1)} %add_rsqrt_fusion.2, f32[1152]{0:T(1024)S(1)} %convert_element_type.97, ...), kind=kOutput, calls=%fused_computation.36 | convolution fusion | flops 3060744192 | bytes 11518464 | tf_op jit(solution)/shard_map/dot_general | solution.py:75
  19.4 0.0 copy-done.7
  19.4 1.6 fusion.10
  21.0 1.7 copy.15
  22.8 2.2 copy.16
  25.0 2.4 fusion.26
  27.5 0.0 all-reduce.3.cloned.1.call-update
  27.5 0.0 all-gather.3.cloned.1.call-start
  27.5 0.7 all-gather.3.cloned.1.call-update
  28.2 0.0 all-gather.5.cloned.1.call-start
  28.3 0.7 all-gather.5.cloned.1.call-update
  29.0 1.8 copy.17
  30.7 0.7 convert_element_type.102
  31.4 1.3 convert_element_type.106
  32.7 89.1 %all-reduce.3.cloned.1.call-done = f32[36,32,32]{1,2,0:T(8,128)} async-done(((f32[36,32,32]{1,2,0:T(8,128)}), f32[36,32,32]{1,2,0:T(8,128)}) %all-reduce.3.cloned.1.call-update) | async-done | bytes 147472 | tf_op jit(solution)/shard_map/psum | solution.py:82
  121.8 2.1 fusion.14
  123.9 0.2 fusion.13
  124.1 0.0 copy-start.5
  124.2 0.0 copy-start.10
  124.2 0.0 copy-start.11
  124.2 0.0 copy-done
  124.2 0.0 copy-done.3
  124.2 2.9 multiply_reduce_fusion
  127.1 101.0 %all-gather.3.cloned.1.call-done = bf16[1152,5760]{1,0:T(8,128)(2,1)} async-done(((bf16[72,5760]{1,0:T(8,128)(2,1)}), bf16[1152,5760]{1,0:T(8,128)(2,1)}) %all-gather.3.cloned.1.call-update) | async-done | bytes 13271056 | tf_op jit(solution)/shard_map/all_gather | solution.py:92
  228.1 0.0 copy-done.5
  228.1 11.6 %multiply_convert_fusion = bf16[384,5760]{1,0:T(8,128)(2,1)S(1)} fusion(bf16[1152,5760]{1,0:T(8,128)(2,1)} %all-gather.3.cloned.1.call-done, f32[5760]{0:T(1024)S(1)} %copy-done.5, f32[384,1152]{1,0:T(8,128)} %get-tuple-element.28, f32[1152]{0:T(1024)S(1)} %copy-done.10, f32[1152]{0:T(1024)S(1)} %copy-done.11, f32[384]{0:T(512)S(1)} %add_rsqrt_fusion), kind=kOutput, calls=%fused_computation.7 | convolution fusion | flops 5111119872 | bytes 19497984 | tf_op jit(solution)/shard_map/dot_general | solution.py:47
  239.7 0.0 copy-start.6
  239.7 0.0 copy-start.4
  239.7 0.2 slice_bitcast_fusion.1
  239.9 2.3 collective-permute-start
  242.2 1.5 collective-permute-start.1
  243.7 0.6 convert_element_type.104
  244.3 1.1 convert_reduce_fusion.8
  245.4 0.0 collective-permute-done
  245.4 1.9 collective-permute-done.1
  247.4 3.0 fusion.5
  250.4 10.6 %multiply_add_fusion = f32[3,128,5760]{2,1,0:T(8,128)S(1)} fusion(bf16[3,128,5760]{2,1,0:T(8,128)(2,1)S(1)} %bitcast.35, bf16[5,130,5760]{2,1,0:T(8,128)(2,1)S(1)} %fusion.5, bf16[1,128,5760]{2,1,0:T(8,128)(2,1)} %copy-done.2, bf16[1,128,5760]{2,1,0:T(8,128)(2,1)S(1)} %collective-permute-done, f32[5760]{0:T(1024)} %get-tuple-element.12, ...), kind=kLoop, calls=%fused_computation.6 | loop fusion | flops 64143360 | bytes 42992640 | tf_op jit(solution)/shard_map/add | solution.py:40
  261.0 2.8 fusion.6
  263.8 46.9 %all-gather.5.cloned.1.call-done = bf16[2880,1152]{0,1:T(8,128)(2,1)} async-done(((bf16[2880,72]{0,1:T(8,128)(2,1)}), bf16[2880,1152]{0,1:T(8,128)(2,1)}) %all-gather.5.cloned.1.call-update) | async-done | bytes 6635536 | tf_op jit(solution)/shard_map/all_gather | solution.py:104
  310.7 0.0 copy-done.9
  310.7 8.4 %fusion.9 = bf16[384,1152]{1,0:T(8,128)(2,1)} fusion(f32[384,1152]{1,0:T(8,128)} %get-tuple-element.28, bf16[384,2880]{1,0:T(8,128)(2,1)} %bitcast.39, bf16[2880,1152]{0,1:T(8,128)(2,1)} %all-gather.5.cloned.1.call-done, f32[1152]{0:T(1024)S(1)} %copy-done.9), kind=kOutput, calls=%fused_computation.18 | convolution fusion | flops 2549366784 | bytes 11506176 | tf_op jit(solution)/shard_map/dot_general | solution.py:102
  (18 shorter events, 0.1 us)
Async XLA Ops:
  6.5 117.6 %copy-start = (bf16[1152,1152]{1,0:T(8,128)(2,1)S(1)}, bf16[1152,1152]{1,0:T(8,128)(2,1)}, u32[]{:S(2)}) copy-start(bf16[1152,1152]{1,0:T(8,128)(2,1)} %param.19) | copy-start | bytes 7962628
  6.5 115.3 %all-reduce.3.cloned.1.call-start = ((), (), s32[]{:S(2)}) async-start(), calls=%async_computation | async-start | bytes 1179648 | tf_op jit(solution)/shard_map/psum | solution.py:82
  10.3 9.1 %copy-start.7 = (f32[384]{0:T(512)}, f32[384]{0:T(512)S(1)}, u32[]{:S(2)}) copy-start(f32[384]{0:T(512)S(1)} %convert_element_type.96) | copy-start | bytes 4612
  27.5 200.6 %all-gather.3.cloned.1.call-start = ((), (), s32[]{:S(2)}) async-start(), calls=%async_computation.1 | async-start | bytes 14100480 | tf_op jit(solution)/shard_map/all_gather | solution.py:92
  28.2 282.4 %all-gather.5.cloned.1.call-start = ((), (), s32[]{:S(2)}) async-start(), calls=%async_computation.2 | async-start | bytes 7206912 | tf_op jit(solution)/shard_map/all_gather | solution.py:104
  121.8 2.4 copy-start.3
  121.8 2.4 copy-start.8
  121.8 2.4 copy-start.12
  124.1 103.9 %copy-start.5 = (f32[5760]{0:T(1024)S(1)}, f32[5760]{0:T(1024)}, u32[]{:S(2)}) copy-start(f32[5760]{0:T(1024)} %convert_element_type.106) | copy-start | bytes 69124
  124.2 103.9 %copy-start.10 = (f32[1152]{0:T(1024)S(1)}, f32[1152]{0:T(1024)}, u32[]{:S(2)}) copy-start(f32[1152]{0:T(1024)} %get-tuple-element.15) | copy-start | bytes 13828
  124.2 103.9 %copy-start.11 = (f32[1152]{0:T(1024)S(1)}, f32[1152]{0:T(1024)}, u32[]{:S(2)}) copy-start(f32[1152]{0:T(1024)} %get-tuple-element.16) | copy-start | bytes 13828
  239.7 4.0 %copy-start.6 = (bf16[5760]{0:T(1024)(128)(2,1)S(1)}, bf16[5760]{0:T(1024)(128)(2,1)}, u32[]{:S(2)}) copy-start(bf16[5760]{0:T(1024)(128)(2,1)} %param.24) | copy-start | bytes 34564
  239.7 4.6 %copy-start.4 = (bf16[3,3,5760]{2,1,0:T(4,128)(2,1)S(1)}, bf16[3,3,5760]{2,1,0:T(4,128)(2,1)}, u32[]{:S(2)}) copy-start(bf16[3,3,5760]{2,1,0:T(4,128)(2,1)} %param.23) | copy-start | bytes 311044
  239.9 5.5 %collective-permute-start = (bf16[1,128,5760]{2,1,0:T(8,128)(2,1)S(1)}, bf16[1,128,5760]{2,1,0:T(8,128)(2,1)S(1)}, u32[]{:S(2)}, u32[]{:S(2)}) collective-permute-start(bf16[1,128,5760]{2,1,0:T(8,128)(2,1)S(1)} %get-tuple-element.20), channel_id=1, source_target_pairs={{0,1},{1,2},{2,3},{3,4},{4,5},{5,6},{6,7},{7,8},{8,9},{9,10},{10,1... | collective-permute-start | bytes 4423688 | tf_op jit(solution)/shard_map/ppermute | solution.py:21
  242.2 5.2 %collective-permute-start.1 = (bf16[1,128,5760]{2,1,0:T(8,128)(2,1)S(1)}, bf16[1,128,5760]{2,1,0:T(8,128)(2,1)S(1)}, u32[]{:S(2)}, u32[]{:S(2)}) collective-permute-start(bf16[1,128,5760]{2,1,0:T(8,128)(2,1)S(1)} %get-tuple-element.21), channel_id=1, source_target_pairs={{1,0},{2,1},{3,2},{4,3},{5,4},{6,5},{7,6},{8,7},{9,8},{10,9},{11,1... | collective-permute-start | bytes 4423688 | tf_op jit(solution)/shard_map/ppermute | solution.py:23
  247.4 3.0 copy-start.2
  261.0 49.7 %copy-start.9 = (f32[1152]{0:T(1024)S(1)}, f32[1152]{0:T(1024)}, u32[]{:S(2)}) copy-start(f32[1152]{0:T(1024)} %get-tuple-element.14) | copy-start | bytes 13828
  310.7 8.4 %copy-start.1 = (bf16[1152,1152]{1,0:T(8,128)(2,1)S(1)}, bf16[1152,1152]{1,0:T(8,128)(2,1)}, u32[]{:S(2)}) copy-start(bf16[1152,1152]{1,0:T(8,128)(2,1)} %param.19) | copy-start | bytes 7962628
Sparse Core Ops, SparseCore 0:
  27.6 94.1 all-reduce.2
  124.0 104.0 all-gather.2
  230.2 80.3 all-gather.4
where the time goes:
time: 326 us
  waiting for transfers between devices  240 us (74%)
  matrix products  34.8 us (11%)
  other arithmetic  26.6 us (8%)
  between operations  14.1 us (4%)
  local copies, waits for them, and re-layouts  5.99 us (2%)
  starting transfers between devices  3.81 us (1%)
    all_gather x1, waiting for transfers between devices, local(): lax.all_gather(in_weight, 'tile', axis=0, tiled=True)  101 us
    psum x1, waiting for transfers between devices, local(): state = lax.psum(local_state, 'tile')  89.1 us
    all_gather x1, waiting for transfers between devices, local(): lax.all_gather(out_weight, 'tile', axis=1, tiled=True)  46.9 us
    dot_general x1, matrix products, row_folder(): return jnp.dot(source, piece, preferred_element_type=jnp.float32)  11.6 us
    add x1, other arithmetic, convolve(): total + window[row_off:row_off + count, col_off:col_off + width, :].astyp...  10.6 us
    dot_general x1, matrix products, local(): jnp.dot(gated, lax.all_gather(out_weight, 'tile', axis=1, tiled=True), pr...  8.36 us
    dot_general x1, matrix products, local(): jnp.dot(normed_in, qkv_weight, preferred_element_type=jnp.float32)  7.45 us
  transfers between devices with their start and end apart: 5, of which 4 were waited for; matrix products, arithmetic and copies ran while one was open for 12% of the time, Pallas kernels for 0%

commit v1 on v0

v1 whole, which is shorter than its diff:
```python
import functools

import jax
import jax.numpy as jnp
from jax import lax
from jax.experimental import pallas as pl
from jax.experimental.pallas import tpu as pltpu
from jax.sharding import PartitionSpec as P

D = 1152
HEADS = 36
HEAD_DIM = 32
FF = 2880
CANVAS_W = 128
LANES = 128
PACK = LANES // HEAD_DIM
GROUPS = D // LANES
MESH = pl.DeviceIdType.MESH


def sum_kernel(n, rows, part_ref, full_ref, landed, mine, send1, recv1, send2, recv2):
    me = lax.axis_index("tile")
    barrier = pltpu.get_barrier_semaphore()

    def greet(k, _):
        pl.semaphore_signal(
            barrier, inc=1, device_id={"tile": lax.rem(me + k, n)}, device_id_type=MESH
        )
        return 0

    lax.fori_loop(1, n, greet, 0)
    pl.semaphore_wait(barrier, n - 1)

    def scatter(k):
        peer = lax.rem(me + k, n)
        return pltpu.make_async_remote_copy(
            src_ref=part_ref.at[peer],
            dst_ref=landed.at[k],
            send_sem=send1.at[k],
            recv_sem=recv1.at[k],
            device_id={"tile": peer},
            device_id_type=MESH,
        )

    def share(k):
        return pltpu.make_async_remote_copy(
            src_ref=mine,
            dst_ref=full_ref.at[me],
            send_sem=send2.at[k],
            recv_sem=recv2.at[k],
            device_id={"tile": lax.rem(me + k, n)},
            device_id_type=MESH,
        )

    def each(do):
        def body(k, _):
            do(k)
            return 0

        lax.fori_loop(1, n, body, 0)

    each(lambda k: scatter(k).start())
    mine[...] = part_ref[me]

    def gather(k):
        scatter(k).wait_recv()
        mine[...] += landed[k]

    each(gather)
    each(lambda k: share(k).start())
    full_ref[me] = mine[...]
    each(lambda k: scatter(k).wait_send())
    each(lambda k: share(k).wait())


def tile_sum(part, n):
    rows = part.shape[1]
    return pl.pallas_call(
        functools.partial(sum_kernel, n, rows),
        out_shape=jax.ShapeDtypeStruct(part.shape, jnp.float32),
        in_specs=[pl.BlockSpec(memory_space=pltpu.VMEM)],
        out_specs=pl.BlockSpec(memory_space=pltpu.VMEM),
        scratch_shapes=[
            pltpu.VMEM((n, rows, LANES), jnp.float32),
            pltpu.VMEM((rows, LANES), jnp.float32),
            pltpu.SemaphoreType.DMA((n,)),
            pltpu.SemaphoreType.DMA((n,)),
            pltpu.SemaphoreType.DMA((n,)),
            pltpu.SemaphoreType.DMA((n,)),
        ],
        compiler_params=pltpu.CompilerParams(collective_id=0, has_side_effects=True),
    )(part)


def modulated_norm(stream, shift, scale):
    factor = lax.rsqrt(jnp.mean(stream * stream, axis=-1, keepdims=True) + 1e-06)
    return stream * factor * (1.0 + scale) + shift


def convolve(window, conv_weight, conv_bias, count):
    width = window.shape[1] - 2
    total = jnp.zeros((count, width, window.shape[2]), jnp.float32) + conv_bias.astype(jnp.float32)
    for row_off in range(3):
        for col_off in range(3):
            total = total + window[row_off : row_off + count, col_off : col_off + width, :].astype(
                jnp.float32
            ) * conv_weight[row_off, col_off].astype(jnp.float32)
    return total


def local(
    n,
    hidden,
    keep_mask,
    kept_embed,
    time_mod,
    timestep,
    qkv_weight,
    proj_weight,
    norm_gain,
    in_weight,
    in_bias,
    conv_weight,
    conv_bias,
    out_weight,
):
    me = lax.axis_index("tile")
    in_full = lax.all_gather(in_weight, "tile", axis=0, tiled=True)
    out_full = lax.all_gather(out_weight, "tile", axis=1, tiled=True)
    modulation = lax.dynamic_index_in_dim(time_mod, timestep[0], 0, keepdims=False).astype(
        jnp.float32
    )
    tokens = hidden.shape[0]
    rows = tokens // CANVAS_W
    stream = (
        hidden.astype(jnp.float32)
        + keep_mask.astype(jnp.float32)[:, None] * kept_embed.astype(jnp.float32)[None, :]
    )
    normed_in = modulated_norm(stream, modulation[0], modulation[1]).astype(jnp.bfloat16)
    mixed_qkv = jnp.dot(normed_in, qkv_weight, preferred_element_type=jnp.float32)
    query = jax.nn.relu(mixed_qkv[:, :D]).astype(jnp.bfloat16)
    key_rows = jax.nn.relu(mixed_qkv[:, D : 2 * D]).astype(jnp.bfloat16)
    values = mixed_qkv[:, 2 * D :].astype(jnp.bfloat16)
    row_head = lax.broadcasted_iota(jnp.int32, (PACK, HEAD_DIM, LANES), 0)
    col_head = lax.broadcasted_iota(jnp.int32, (PACK, HEAD_DIM, LANES), 2) // HEAD_DIM
    same = (row_head == col_head).astype(jnp.float32)
    packed = []
    for g in range(GROUPS):
        cols = slice(g * LANES, (g + 1) * LANES)
        outer = lax.dot_general(
            key_rows[:, cols],
            values[:, cols],
            (((0,), (0,)), ((), ())),
            preferred_element_type=jnp.float32,
        )
        packed.append(jnp.sum(outer.reshape(PACK, HEAD_DIM, LANES) * same, axis=0))
    part = jnp.concatenate(packed, axis=0)
    used = part.shape[0]
    per = -(-used // (8 * n)) * 8
    part = jnp.pad(part, ((0, per * n - used), (0, 0))).reshape(n, per, LANES)
    state = tile_sum(part, n).reshape(n * per, LANES)
    pieces = []
    for g in range(GROUPS):
        block = (state[g * HEAD_DIM : (g + 1) * HEAD_DIM][None] * same).reshape(LANES, LANES)
        pieces.append(
            jnp.dot(
                query[:, g * LANES : (g + 1) * LANES].astype(jnp.float32),
                block,
                precision=lax.Precision.HIGHEST,
            )
        )
    attended = jnp.concatenate(pieces, axis=1)
    factor = lax.rsqrt(jnp.mean(attended * attended, axis=-1, keepdims=True) + 1e-06)
    normed_attn = (attended * factor * norm_gain.astype(jnp.float32)).astype(jnp.bfloat16)
    after_attn = stream + modulation[2] * jnp.dot(
        normed_attn, proj_weight, preferred_element_type=jnp.float32
    )
    normed_ffn = modulated_norm(after_attn, modulation[3], modulation[4]).astype(jnp.bfloat16)
    down = [(i, i + 1) for i in range(n - 1)]
    up = [(i + 1, i) for i in range(n - 1)]
    above = lax.ppermute(normed_ffn[tokens - CANVAS_W :], "tile", down)
    below = lax.ppermute(normed_ffn[:CANVAS_W], "tile", up)
    framed = jnp.concatenate([above, normed_ffn, below], axis=0)
    before = jnp.dot(framed, in_full, preferred_element_type=jnp.float32)
    inner = (
        jax.nn.silu(before + in_bias.astype(jnp.float32))
        .astype(jnp.bfloat16)
        .reshape(rows + 2, CANVAS_W, 2 * FF)
    )
    row_id = lax.broadcasted_iota(jnp.int32, (rows + 2, 1, 1), 0)
    inside = ((row_id > 0) | (me > 0)) & ((row_id < rows + 1) | (me < n - 1))
    inner = jnp.where(inside, inner, jnp.zeros_like(inner))
    padded = jnp.pad(inner, ((0, 0), (1, 1), (0, 0)))
    conv = convolve(padded, conv_weight, conv_bias, rows)
    gated = (conv[..., :FF] * jax.nn.silu(conv[..., FF:])).astype(jnp.bfloat16).reshape(tokens, FF)
    projected = jnp.dot(gated, out_full, preferred_element_type=jnp.float32)
    return (after_attn + modulation[5] * projected).astype(jnp.bfloat16)


def solution(mesh):
    in_specs = (
        P(("groups", "tile"), None),
        P(("groups", "tile")),
        P(),
        P(),
        P("groups"),
        P(),
        P(),
        P(),
        P("tile", None),
        P(),
        P(),
        P(),
        P(None, "tile"),
    )
    return jax.shard_map(
        functools.partial(local, mesh.shape["tile"]),
        mesh=mesh,
        in_specs=in_specs,
        out_specs=P(("groups", "tile"), None),
        check_vma=False,
    )
```

time: 326 us -> 213 us (0.65)
  waiting for transfers between devices: 240 us -> 99.8 us
  Pallas kernels: 0 us -> 23.8 us
  matrix products: 34.8 us -> 39.8 us
    psum x1 -> x0, waiting for transfers between devices: 89.1 us -> none  [local(): state = lax.psum(local_state, 'tile')]
    all_gather x2, waiting for transfers between devices: 148 us -> 95.4 us  [the longest x1 65.1 us: local(): in_full = lax.all_gather(in_weight, 'tile', axis=0, tiled=True)]
    pallas_call x0 -> x1, Pallas kernels: none -> 23.8 us  [tile_sum(): pl.pallas_call(functools.partial(sum_kernel, n, rows), out_shape=jax.Shap...]
    dot_general x4 -> x20, matrix products: 24.5 us -> 30.5 us  [the longest x1 17.6 us: local(): before = jnp.dot(framed, in_full, preferred_element_type=jnp.float32)]
    select_n x0 -> x1, other arithmetic: none -> 3.79 us  [local(): inner = jnp.where(inside, inner, jnp.zeros_like(inner))]
    convert_element_type x2 -> x0, local copies, waits for them, and re-layouts: 3.5 us -> none  [the longest x1 1.76 us: local(): jax.nn.relu(mixed_qkv[:, :D]).astype(jnp.bfloat16)]
  transfers between devices with their start and end apart: 5 -> 4, of which waited for: 4 -> 3; matrix products, arithmetic and copies ran while one was open for 12% -> 28% of each run, Pallas kernels for 0% -> 11%
where the time goes in v1:
time: 213 us; the launch traced here: 212 us
  waiting for transfers between devices  99.8 us (47%)
  matrix products  39.8 us (19%)
  other arithmetic  24.9 us (12%)
  Pallas kernels  23.8 us (11%)
  between operations  14.6 us (7%)
  local copies, waits for them, and re-layouts  5.27 us (2%)
  starting transfers between devices  4.37 us (2%)
    all_gather x1, waiting for transfers between devices, local(): in_full = lax.all_gather(in_weight, 'tile', axis=0, tiled=True)  65.1 us
    all_gather x1, waiting for transfers between devices, local(): out_full = lax.all_gather(out_weight, 'tile', axis=1, tiled=True)  30.3 us
    pallas_call x1, Pallas kernels, tile_sum(): pl.pallas_call(functools.partial(sum_kernel, n, rows), out_shape=jax.Shap...  23.8 us
    dot_general x1, matrix products, local(): before = jnp.dot(framed, in_full, preferred_element_type=jnp.float32)  17.6 us
    add x1, other arithmetic, convolve(): total + window[row_off:row_off + count, col_off:col_off + width, :].astyp...  10.5 us
    dot_general x1, matrix products, local(): projected = jnp.dot(gated, out_full, preferred_element_type=jnp.float32)  8.36 us
    dot_general x1, matrix products, local(): jnp.dot(normed_in, qkv_weight, preferred_element_type=jnp.float32)  7.45 us
  transfers between devices with their start and end apart: 4, of which 3 were waited for; matrix products, arithmetic and copies ran while one was open for 28% of the time, Pallas kernels for 11%

profile of v1, /device:TPU:0, one launch (start us, length us, event | category | flops | bytes accessed | tf_op | source)
XLA Modules:
  0.0 212.5 jit_solution(9157011466749627855)
XLA Ops:
  6.5 0.7 all-gather.3.cloned.1.call-update
  7.3 0.7 all-gather.5.cloned.1.call-update
  8.7 0.9 dynamic-slice_convert_fusion
  9.6 0.7 slice_reduce_fusion.1
  10.2 0.7 convert_element_type.108
  10.9 0.7 convert_element_type.107
  11.6 1.6 multiply_reduce_fusion.2
  13.2 7.4 %fusion.11 = bf16[384,3456]{1,0:T(8,128)(2,1)S(1)} fusion(bf16[1152,3456]{1,0:T(8,128)(2,1)} %param.18, bf16[384,1152]{1,0:T(8,128)(2,1)} %param.13, f32[1152]{0:T(1024)S(1)} %get-tuple-element.17, f32[1152]{0:T(1024)S(1)} %get-tuple-element.18, f32[384]{0:T(512)S(1)} %add_rsqrt_fusion.2, f32[1152]{0:T(1024)S(1)} %convert_element_type.108, ...), kind=kOutput, calls=%fused_computation.39 | convolution fusion | flops 3060744192 | bytes 11518464 | tf_op jit(solution)/shard_map/dot_general | solution.py:140
  20.7 0.3 fusion.5
  21.0 0.2 fusion.51
  21.2 0.2 fusion.48
  21.4 0.2 fusion.45
  21.7 0.2 fusion.42
  21.9 0.2 fusion.39
  22.1 0.2 fusion.36
  22.3 0.2 fusion.33
  22.5 0.2 fusion.30
  22.7 0.2 fusion.27
  23.2 0.7 pad.8
  23.9 23.8 %shard_map.127 = f32[16,24,128]{2,1,0:T(8,128)} custom-call(f32[16,24,128]{2,1,0:T(8,128)} %bitcast.51), custom_call_target="tpu_custom_call" | custom-call | tf_op jit(solution)/shard_map/pallas_call | solution.py:78
  47.7 1.5 fusion.59
  49.2 0.5 iota.247
  49.8 1.2 iota.248
  51.0 0.7 convert_element_type.113
  51.7 1.0 bitcast_select_fusion
  52.7 0.3 convolution_dynamic-update-slice_fusion.8
  53.0 0.3 convolution_dynamic-update-slice_fusion.7
  53.3 0.3 convolution_dynamic-update-slice_fusion.6
  53.6 0.3 convolution_dynamic-update-slice_fusion.5
  53.9 0.3 convolution_dynamic-update-slice_fusion.4
  54.2 0.3 convolution_dynamic-update-slice_fusion.3
  54.5 0.3 convolution_dynamic-update-slice_fusion.2
  54.8 0.3 convolution_dynamic-update-slice_fusion.1
  55.1 0.3 convolution_dynamic-update-slice_fusion
  55.7 1.9 multiply_reduce_fusion
  57.6 1.1 copy-done.2
  58.8 0.3 add_convert_fusion
  59.1 2.9 %collective-permute-start = (bf16[128,1152]{1,0:T(8,128)(2,1)S(1)}, bf16[128,1152]{1,0:T(8,128)(2,1)S(1)}, u32[]{:S(2)}, u32[]{:S(2)}) collective-permute-start(bf16[128,1152]{1,0:T(8,128)(2,1)S(1)} %get-tuple-element.31), channel_id=1, source_target_pairs={{0,1},{1,2},{2,3},{3,4},{4,5},{5,6},{6,7},{7,8},{8,9},{9,10},{10,1... | collective-permute-start | bytes 884744 | tf_op jit(solution)/shard_map/ppermute | solution.py:181
  62.0 1.5 collective-permute-start.1
  63.5 0.5 convert_reduce_fusion.8
  64.1 3.0 %collective-permute-done.1 = bf16[128,1152]{1,0:T(8,128)(2,1)S(1)} collective-permute-done((bf16[128,1152]{1,0:T(8,128)(2,1)S(1)}, bf16[128,1152]{1,0:T(8,128)(2,1)S(1)}, u32[]{:S(2)}, u32[]{:S(2)}) %collective-permute-start.1) | collective-permute-done | bytes 294944 | tf_op jit(solution)/shard_map/ppermute | solution.py:182
  67.1 65.1 %all-gather.3.cloned.1.call-done = bf16[1152,5760]{1,0:T(8,128)(2,1)} async-done(((bf16[72,5760]{1,0:T(8,128)(2,1)}), bf16[1152,5760]{1,0:T(8,128)(2,1)}) %all-gather.3.cloned.1.call-update) | async-done | bytes 13271056 | tf_op jit(solution)/shard_map/all_gather | solution.py:128
  132.1 17.6 %multiply_convert_fusion = bf16[640,5760]{1,0:T(8,128)(2,1)} fusion(bf16[1152,5760]{1,0:T(8,128)(2,1)} %all-gather.3.cloned.1.call-done, f32[5760]{0:T(1024)S(1)} %convert_element_type.117, bf16[128,1152]{1,0:T(8,128)(2,1)S(1)} %collective-permute-done.1, bf16[384,1152]{1,0:T(8,128)(2,1)S(1)} %add_convert_fusion, bf16[128,1152]{1,0:T(8,128)(2,1)S(1)} %collective-permute-done), kind=kOutput, calls=%fused_computation | convolution fusion | flops 8520007680 | bytes 22141440 | tf_op jit(solution)/shard_map/dot_general | solution.py:184
  149.7 3.8 %broadcast_select_fusion = bf16[5,128,5760]{2,1,0:T(8,128)(2,1)S(1)} fusion(bf16[5,128,5760]{2,1,0:T(8,128)(2,1)} %bitcast.49, pred[5]{0:T(512)(128)(4,1)S(1)} %or_and_fusion), kind=kLoop, calls=%fused_computation.2 | loop fusion | flops 3686400 | bytes 14745605 | tf_op jit(solution)/shard_map/jit(_where)/select_n | solution.py:192
  153.5 10.5 %multiply_add_fusion = f32[3,128,5760]{2,1,0:T(8,128)S(1)} fusion(bf16[5,128,5760]{2,1,0:T(8,128)(2,1)S(1)} %broadcast_select_fusion, f32[5760]{0:T(1024)S(1)} %get-tuple-element.12, f32[5760]{0:T(1024)S(1)} %get-tuple-element.13, f32[5760]{0:T(1024)S(1)} %get-tuple-element.6, f32[5760]{0:T(1024)S(1)} %get-tuple-element.7, f32[5760]{0:T(1024)S(1)} %get-tuple-element.8, ...), kind=kLoop, calls=%fused_computation.1 | loop fusion | flops 59719680 | bytes 29736960 | tf_op jit(solution)/shard_map/add | solution.py:105
  164.0 2.9 %fusion = bf16[3,128,2880]{2,1,0:T(8,128)(2,1)} fusion(f32[3,128,5760]{2,1,0:T(8,128)S(1)} %multiply_add_fusion), kind=kLoop, calls=%fused_computation.4 | loop fusion | flops 6635520 | bytes 11059200 | tf_op jit(solution)/shard_map/convert_element_type | solution.py:195
  166.9 30.3 %all-gather.5.cloned.1.call-done = bf16[2880,1152]{0,1:T(8,128)(2,1)} async-done(((bf16[2880,72]{0,1:T(8,128)(2,1)}), bf16[2880,1152]{0,1:T(8,128)(2,1)}) %all-gather.5.cloned.1.call-update) | async-done | bytes 6635536 | tf_op jit(solution)/shard_map/all_gather | solution.py:129
  197.3 8.4 %fusion.3 = bf16[384,1152]{1,0:T(8,128)(2,1)} fusion(f32[384,1152]{1,0:T(8,128)} %copy-done.2, bf16[384,2880]{1,0:T(8,128)(2,1)} %bitcast.50, bf16[2880,1152]{0,1:T(8,128)(2,1)} %all-gather.5.cloned.1.call-done, f32[1152]{0:T(1024)S(1)} %copy-done.11), kind=kOutput, calls=%fused_computation.13 | convolution fusion | flops 2549366784 | bytes 11506176 | tf_op jit(solution)/shard_map/dot_general | solution.py:196
  (52 shorter events, 0.5 us)
Async XLA Ops:
  6.5 49.1 %copy-start = (bf16[1152,1152]{1,0:T(8,128)(2,1)S(1)}, bf16[1152,1152]{1,0:T(8,128)(2,1)}, u32[]{:S(2)}) copy-start(bf16[1152,1152]{1,0:T(8,128)(2,1)} %param.19) | copy-start | bytes 7962628
  6.5 125.6 %all-gather.3.cloned.1.call-start = ((), (), s32[]{:S(2)}) async-start(), calls=%async_computation | async-start | bytes 14100480 | tf_op jit(solution)/shard_map/all_gather | solution.py:128
  7.3 190.0 %all-gather.5.cloned.1.call-start = ((), (), s32[]{:S(2)}) async-start(), calls=%async_computation.1 | async-start | bytes 7206912 | tf_op jit(solution)/shard_map/all_gather | solution.py:129
  11.6 9.1 %copy-start.5 = (f32[384]{0:T(512)}, f32[384]{0:T(512)S(1)}, u32[]{:S(2)}) copy-start(f32[384]{0:T(512)S(1)} %convert_element_type.107) | copy-start | bytes 4612
  23.0 0.9 copy-start.12
  23.0 0.9 copy-start.13
  23.0 0.9 copy-start.14
  52.7 3.0 %copy-start.3 = (bf16[384,1152]{1,0:T(8,128)(2,1)S(1)}, bf16[384,1152]{1,0:T(8,128)(2,1)}, u32[]{:S(2)}) copy-start(bf16[384,1152]{1,0:T(8,128)(2,1)} %param.13) | copy-start | bytes 2654212
  52.7 3.0 %copy-start.6 = (f32[384]{0:T(512)S(1)}, f32[384]{0:T(512)}, u32[]{:S(2)}) copy-start(f32[384]{0:T(512)} %copy-done.5) | copy-start | bytes 4612
  55.7 3.1 %copy-start.7 = (f32[1152]{0:T(1024)S(1)}, f32[1152]{0:T(1024)}, u32[]{:S(2)}) copy-start(f32[1152]{0:T(1024)} %get-tuple-element.15) | copy-start | bytes 13828
  55.7 3.1 %copy-start.8 = (f32[1152]{0:T(1024)S(1)}, f32[1152]{0:T(1024)}, u32[]{:S(2)}) copy-start(f32[1152]{0:T(1024)} %get-tuple-element.16) | copy-start | bytes 13828
  57.5 1.2 copy-start.2
  57.6 5.9 %copy-start.9 = (bf16[5760]{0:T(1024)(128)(2,1)S(1)}, bf16[5760]{0:T(1024)(128)(2,1)}, u32[]{:S(2)}) copy-start(bf16[5760]{0:T(1024)(128)(2,1)} %param.22) | copy-start | bytes 34564
  57.6 5.9 %copy-start.10 = (bf16[5760]{0:T(1024)(128)(2,1)S(1)}, bf16[5760]{0:T(1024)(128)(2,1)}, u32[]{:S(2)}) copy-start(bf16[5760]{0:T(1024)(128)(2,1)} %param.24) | copy-start | bytes 34564
  57.6 5.9 %copy-start.4 = (bf16[3,3,5760]{2,1,0:T(4,128)(2,1)S(1)}, bf16[3,3,5760]{2,1,0:T(4,128)(2,1)}, u32[]{:S(2)}) copy-start(bf16[3,3,5760]{2,1,0:T(4,128)(2,1)} %param.23) | copy-start | bytes 311044
  59.1 5.0 %collective-permute-start = (bf16[128,1152]{1,0:T(8,128)(2,1)S(1)}, bf16[128,1152]{1,0:T(8,128)(2,1)S(1)}, u32[]{:S(2)}, u32[]{:S(2)}) collective-permute-start(bf16[128,1152]{1,0:T(8,128)(2,1)S(1)} %get-tuple-element.31), channel_id=1, source_target_pairs={{0,1},{1,2},{2,3},{3,4},{4,5},{5,6},{6,7},{7,8},{8,9},{9,10},{10,1... | collective-permute-start | bytes 884744 | tf_op jit(solution)/shard_map/ppermute | solution.py:181
  62.0 5.1 %collective-permute-start.1 = (bf16[128,1152]{1,0:T(8,128)(2,1)S(1)}, bf16[128,1152]{1,0:T(8,128)(2,1)S(1)}, u32[]{:S(2)}, u32[]{:S(2)}) collective-permute-start(bf16[128,1152]{1,0:T(8,128)(2,1)S(1)} %get-tuple-element.32), channel_id=1, source_target_pairs={{1,0},{2,1},{3,2},{4,3},{5,4},{6,5},{7,6},{8,7},{9,8},{10,9},{11,1... | collective-permute-start | bytes 884744 | tf_op jit(solution)/shard_map/ppermute | solution.py:182
  164.0 33.3 %copy-start.11 = (f32[1152]{0:T(1024)S(1)}, f32[1152]{0:T(1024)}, u32[]{:S(2)}) copy-start(f32[1152]{0:T(1024)} %get-tuple-element.14) | copy-start | bytes 13828
  197.3 8.4 %copy-start.1 = (bf16[1152,1152]{1,0:T(8,128)(2,1)S(1)}, bf16[1152,1152]{1,0:T(8,128)(2,1)}, u32[]{:S(2)}) copy-start(bf16[1152,1152]{1,0:T(8,128)(2,1)} %param.19) | copy-start | bytes 7962628
Sparse Core Ops, SparseCore 0:
  9.5 122.5 all-gather.2
  134.3 62.9 all-gather.4

commit v2 on v1

v2 whole, which is shorter than its diff:
```python
import functools

import jax
import jax.numpy as jnp
from jax import lax
from jax.experimental import pallas as pl
from jax.experimental.pallas import tpu as pltpu
from jax.sharding import PartitionSpec as P

D = 1152
HEADS = 36
HEAD_DIM = 32
FF = 2880
CANVAS_W = 128
LANES = 128
PACK = LANES // HEAD_DIM
GROUPS = D // LANES
MESH = pl.DeviceIdType.MESH


def mesh_box(n):
    wide = 1
    while (2 * wide) ** 2 <= n // 2:
        wide *= 2
    return n // (2 * wide), wide


def front_kernel(
    n,
    hidden_ref,
    mask_ref,
    embed_ref,
    mod_ref,
    qkv_ref,
    proj_ref,
    gain_ref,
    shard_ref,
    full_ref,
    after_ref,
    frame_ref,
    mixed,
    part,
    landed,
    mine,
    state,
    normed,
    send1,
    recv1,
    send2,
    recv2,
    halo_send,
    halo_recv,
    line_send,
    side_send,
    group_send,
    core_send,
    arrive,
    sibling,
    own_sem,
):
    count_a, count_b = mesh_box(n)
    me = lax.axis_index("tile")
    plane = lax.axis_index("groups")
    core = lax.rem(me, 2)
    at_b = lax.rem(me // 2, count_b)
    at_a = me // (2 * count_b)
    rows = shard_ref.shape[0]
    cut = -(-rows // 16) * 8
    rows_of = (slice(0, cut), slice(cut, rows))
    per = mine.shape[0]
    tokens = hidden_ref.shape[0]

    def tile_of(a, b, c):
        return (a * count_b + b) * 2 + c

    barrier = pltpu.get_barrier_semaphore()

    def greet(k, _):
        pl.semaphore_signal(
            barrier, inc=1, device_id={"tile": lax.rem(me + k, n)}, device_id_type=MESH
        )
        return 0

    lax.fori_loop(1, n, greet, 0)
    pl.semaphore_signal(barrier, inc=1, device_id={"groups": 1 - plane}, device_id_type=MESH)
    pl.semaphore_wait(barrier, n)

    def place(a, b, c, p):
        return full_ref.at[tile_of(a, b, c), rows_of[p]]

    def remote(src, a, b, p, send, recv, target):
        return pltpu.make_async_remote_copy(
            src_ref=src,
            dst_ref=place(a, b, core, p),
            send_sem=send,
            recv_sem=recv.at[a, b, p],
            device_id=target,
            device_id_type=MESH,
        )

    def source(a, b, p, own):
        return shard_ref.at[rows_of[p]] if own else place(a, b, core, p)

    def line(a, p, way, own=False):
        return remote(
            source(a, at_b, p, own),
            a,
            at_b,
            p,
            line_send.at[way, a, p],
            arrive,
            {"tile": tile_of(at_a + (1 if way == 0 else -1), at_b, core)},
        )

    def side(a, k, p, own=False):
        return remote(
            source(a, at_b, p, own),
            a,
            at_b,
            p,
            side_send.at[k, a],
            arrive,
            {"tile": tile_of(at_a, lax.rem(at_b + k, count_b), core)},
        )

    def group(a, b, p):
        return remote(
            source(a, b, p, False),
            a,
            b,
            p,
            group_send.at[a, b],
            arrive,
            {"groups": 1 - plane},
        )

    def twin(a, b, p, own=False):
        return remote(
            source(a, b, p, own),
            a,
            b,
            p,
            core_send.at[a, b, p],
            sibling,
            {"tile": tile_of(at_a, at_b, 1 - core)},
        )

    def arrived(a, b, p, recv=arrive, c=None):
        ref = place(a, b, core if c is None else c, p)
        pltpu.make_async_remote_copy(
            src_ref=ref,
            dst_ref=ref,
            send_sem=own_sem,
            recv_sem=recv.at[a, b, p],
            device_id={"tile": tile_of(at_a, at_b, 1 - core)},
            device_id_type=MESH,
        ).wait_recv()

    ways = ((at_a < count_a - 1), (at_a > 0))
    keep = pltpu.make_async_copy(shard_ref, full_ref.at[me], own_sem)
    keep.start()
    for p in range(2):
        for way in range(2):
            @pl.when(ways[way])
            def _():
                line(at_a, p, way, True).start()

        @pl.when(plane == p)
        def _():
            for k in range(1, count_b):
                side(at_a, k, p, True).start()

        twin(at_a, at_b, p, True).start()

    stream = hidden_ref[...].astype(jnp.float32) + mask_ref[...] * embed_ref[...]
    normed[...] = modulated_norm(stream, mod_ref[0:1, :], mod_ref[1:2, :]).astype(jnp.bfloat16)
    after_ref[...] = stream
    span = D // 3

    def project(j, _):
        cols = pl.ds(pl.multiple_of(j * span, LANES), span)
        out = jnp.dot(normed[...], qkv_ref[:, cols], preferred_element_type=jnp.float32)
        out = jnp.where(j < 6, jnp.maximum(out, 0.0), out)
        mixed[:, cols] = out.astype(jnp.bfloat16)
        return 0

    lax.fori_loop(0, 9, project, 0)
    row_head = lax.broadcasted_iota(jnp.int32, (LANES, LANES), 0) // HEAD_DIM
    col_head = lax.broadcasted_iota(jnp.int32, (LANES, LANES), 1) // HEAD_DIM
    same = row_head == col_head
    part[...] = jnp.zeros_like(part)

    def outer(g, _):
        first = pl.multiple_of(g * LANES, LANES)
        product = lax.dot_general(
            mixed[:, pl.ds(D + first, LANES)],
            mixed[:, pl.ds(2 * D + first, LANES)],
            (((0,), (0,)), ((), ())),
            preferred_element_type=jnp.float32,
        )
        product = jnp.where(same, product, 0.0)
        packed = product[:HEAD_DIM]
        for h in range(1, PACK):
            packed = packed + product[h * HEAD_DIM : (h + 1) * HEAD_DIM]
        part[pl.ds(pl.multiple_of(g * HEAD_DIM, HEAD_DIM), HEAD_DIM), :] = packed
        return 0

    lax.fori_loop(0, GROUPS, outer, 0)

    def slot(ref, k):
        return ref.at[pl.ds(pl.multiple_of(k * per, 8), per)]

    def scatter(k):
        peer = lax.rem(me + k, n)
        return pltpu.make_async_remote_copy(
            src_ref=slot(part, peer),
            dst_ref=landed.at[k],
            send_sem=send1.at[k],
            recv_sem=recv1.at[k],
            device_id={"tile": peer},
            device_id_type=MESH,
        )

    def share(k):
        return pltpu.make_async_remote_copy(
            src_ref=mine,
            dst_ref=slot(state, me),
            send_sem=send2.at[k],
            recv_sem=recv2.at[k],
            device_id={"tile": lax.rem(me + k, n)},
            device_id_type=MESH,
        )

    def each(do):
        def body(k, _):
            do(k)
            return 0

        lax.fori_loop(1, n, body, 0)

    each(lambda k: scatter(k).start())
    mine[...] = part[pl.ds(pl.multiple_of(me * per, 8), per), :]

    def gather(k):
        scatter(k).wait_recv()
        mine[...] += landed[k]

    each(gather)
    each(lambda k: share(k).start())
    state[pl.ds(pl.multiple_of(me * per, 8), per), :] = mine[...]
    each(lambda k: scatter(k).wait_send())
    each(lambda k: share(k).wait())

    pieces = []
    for g in range(GROUPS):
        block = jnp.concatenate([state[g * HEAD_DIM : (g + 1) * HEAD_DIM, :]] * PACK, axis=0)
        block = jnp.where(same, block, 0.0)
        pieces.append(
            jnp.dot(
                mixed[:, g * LANES : (g + 1) * LANES].astype(jnp.float32),
                block,
                precision=lax.Precision.HIGHEST,
                preferred_element_type=jnp.float32,
            )
        )
    attended = jnp.concatenate(pieces, axis=1)
    factor = lax.rsqrt(jnp.mean(attended * attended, axis=-1, keepdims=True) + 1e-06)
    normed[...] = (attended * factor * gain_ref[...]).astype(jnp.bfloat16)

    def attach(j, _):
        cols = pl.ds(pl.multiple_of(j * span, LANES), span)
        out = jnp.dot(normed[...], proj_ref[:, cols], preferred_element_type=jnp.float32)
        after_ref[:, cols] += mod_ref[2:3, cols] * out
        return 0

    lax.fori_loop(0, 3, attach, 0)
    frame_ref[CANVAS_W : CANVAS_W + tokens, :] = modulated_norm(
        after_ref[...], mod_ref[3:4, :], mod_ref[4:5, :]
    ).astype(jnp.bfloat16)

    def halo(way):
        lo = tokens if way == 0 else CANVAS_W
        to = 0 if way == 0 else CANVAS_W + tokens
        return pltpu.make_async_remote_copy(
            src_ref=frame_ref.at[lo : lo + CANVAS_W],
            dst_ref=frame_ref.at[to : to + CANVAS_W],
            send_sem=halo_send.at[way],
            recv_sem=halo_recv.at[way],
            device_id={"tile": me + (1 if way == 0 else -1)},
            device_id_type=MESH,
        )

    has = (me < n - 1, me > 0)
    for way in range(2):
        @pl.when(has[way])
        def _():
            halo(way).start()

    @pl.when(me == 0)
    def _():
        frame_ref[:CANVAS_W, :] = jnp.zeros((CANVAS_W, D), jnp.bfloat16)

    @pl.when(me == n - 1)
    def _():
        frame_ref[CANVAS_W + tokens :, :] = jnp.zeros((CANVAS_W, D), jnp.bfloat16)

    def near(d):
        if d == 0:
            return [(at_a, None, 0)]
        return [(at_a - d, at_a >= d, 0), (at_a + d, at_a < count_a - d, 1)]

    def under(cond, do):
        if cond is None:
            do()
        else:
            pl.when(cond)(do)

    for stage in range(1, count_a + 2):
        for a, ok, way in near(stage) if stage < count_a else []:
            def from_line(a=a, way=way):
                for p in range(2):
                    arrived(a, at_b, p)

                    @pl.when(ways[way])
                    def _():
                        line(a, p, way).start()

                    @pl.when(plane == p)
                    def _():
                        for k in range(1, count_b):
                            side(a, k, p).start()

                    twin(a, at_b, p).start()

            under(ok, from_line)
        for a, ok, way in near(stage - 1) if stage - 1 < count_a else []:
            def from_side(a=a):
                for k in range(1, count_b):
                    b = lax.rem(at_b + k, count_b)
                    for p in range(2):
                        @pl.when(plane == p)
                        def _():
                            arrived(a, b, p)
                            group(a, b, p).start()
                            twin(a, b, p).start()

            under(ok, from_side)
        for a, ok, way in near(stage - 2) if 0 <= stage - 2 < count_a else []:
            def from_group(a=a):
                for k in range(1, count_b):
                    b = lax.rem(at_b + k, count_b)
                    for p in range(2):
                        @pl.when(plane != p)
                        def _():
                            arrived(a, b, p)
                            twin(a, b, p).start()

            under(ok, from_group)

    keep.wait()
    for way in range(2):
        @pl.when(has[way])
        def _():
            halo(way).wait_send()

        @pl.when(has[1 - way])
        def _():
            halo(way).wait_recv()

    for a in range(count_a):
        for p in range(2):
            @pl.when(jnp.logical_and(ways[0], at_a >= a))
            def _():
                line(a, p, 0).wait_send()

            @pl.when(jnp.logical_and(ways[1], at_a <= a))
            def _():
                line(a, p, 1).wait_send()

            @pl.when(plane == p)
            def _():
                for k in range(1, count_b):
                    side(a, k, p).wait_send()
                    group(a, lax.rem(at_b + k, count_b), p).wait_send()

            for b in range(count_b):
                twin(a, b, p).wait_send()
                arrived(a, b, p, sibling, 1 - core)


def front(hidden, mask, embed, mod, qkv_weight, proj_weight, gain, shard, n):
    count_a, count_b = mesh_box(n)
    tokens = hidden.shape[0]
    per = -(-GROUPS * HEAD_DIM // (8 * n)) * 8
    vmem = pl.BlockSpec(memory_space=pltpu.VMEM)
    dma = pltpu.SemaphoreType.DMA
    return pl.pallas_call(
        functools.partial(front_kernel, n),
        out_shape=(
            jax.ShapeDtypeStruct((n,) + shard.shape, jnp.bfloat16),
            jax.ShapeDtypeStruct((tokens, D), jnp.float32),
            jax.ShapeDtypeStruct((tokens + 2 * CANVAS_W, D), jnp.bfloat16),
        ),
        in_specs=[vmem] * 7 + [pl.BlockSpec(memory_space=pl.ANY)],
        out_specs=(pl.BlockSpec(memory_space=pl.ANY), vmem, vmem),
        scratch_shapes=[
            pltpu.VMEM((tokens, 3 * D), jnp.bfloat16),
            pltpu.VMEM((n * per, LANES), jnp.float32),
            pltpu.VMEM((n, per, LANES), jnp.float32),
            pltpu.VMEM((per, LANES), jnp.float32),
            pltpu.VMEM((n * per, LANES), jnp.float32),
            pltpu.VMEM((tokens, D), jnp.bfloat16),
            dma((n,)),
            dma((n,)),
            dma((n,)),
            dma((n,)),
            dma((2,)),
            dma((2,)),
            dma((2, count_a, 2)),
            dma((count_b, count_a)),
            dma((count_a, count_b)),
            dma((count_a, count_b, 2)),
            dma((count_a, count_b, 2)),
            dma((count_a, count_b, 2)),
            dma,
        ],
        compiler_params=pltpu.CompilerParams(
            collective_id=0, has_side_effects=True, vmem_limit_bytes=50 << 20
        ),
    )(hidden, mask, embed, mod, qkv_weight, proj_weight, gain, shard)


def modulated_norm(stream, shift, scale):
    factor = lax.rsqrt(jnp.mean(stream * stream, axis=-1, keepdims=True) + 1e-06)
    return stream * factor * (1.0 + scale) + shift


def silu(v):
    half = 0.5 * v
    return half * (1.0 + jnp.tanh(half))


def ffn_kernel(
    edge_ref,
    x_ref,
    wa_ref,
    wb_ref,
    wo_ref,
    pa_ref,
    pb_ref,
    base_ref,
    gate_ref,
    out_ref,
    acc_ref,
):
    step = pl.program_id(0)
    frame = x_ref.shape[0]
    tokens = frame - 2 * CANVAS_W
    x = x_ref[...]
    column = lax.broadcasted_iota(jnp.int32, (CANVAS_W, LANES), 0)
    not_left = column > 0
    not_right = column < CANVAS_W - 1

    def filtered(w_ref, p_ref):
        v = jnp.dot(x, w_ref[...], preferred_element_type=jnp.float32) + p_ref[10:11, :]
        e = silu(v).astype(jnp.bfloat16).astype(jnp.float32)
        lines = [e[r * CANVAS_W : (r + 1) * CANVAS_W] for r in range(frame // CANVAS_W)]
        lines[0] = lines[0] * edge_ref[0]
        lines[-1] = lines[-1] * edge_ref[1]
        out = []
        for r in range(tokens // CANVAS_W):
            side = []
            for j in range(3):
                side.append(
                    lines[r] * p_ref[j : j + 1, :]
                    + lines[r + 1] * p_ref[3 + j : 4 + j, :]
                    + lines[r + 2] * p_ref[6 + j : 7 + j, :]
                )
            left = jnp.where(not_left, pltpu.roll(side[0], 1, 0), 0.0)
            right = jnp.where(not_right, pltpu.roll(side[2], CANVAS_W - 1, 0), 0.0)
            out.append(left + side[1] + right + p_ref[9:10, :])
        return out

    first_half = filtered(wa_ref, pa_ref)
    second_half = filtered(wb_ref, pb_ref)
    gated = jnp.concatenate(
        [(a * silu(b)).astype(jnp.bfloat16) for a, b in zip(first_half, second_half)], axis=0
    )
    part = lax.dot_general(
        gated, wo_ref[...], (((1,), (1,)), ((), ())), preferred_element_type=jnp.float32
    )

    @pl.when(step == 0)
    def _():
        acc_ref[...] = part

    @pl.when(step > 0)
    def _():
        acc_ref[...] += part

    @pl.when(step == pl.num_programs(0) - 1)
    def _():
        out_ref[...] = (base_ref[...] + gate_ref[...] * acc_ref[...]).astype(out_ref.dtype)


def ffn(x, edges, weights, params, base, gate, dtype):
    count = weights.shape[1] // (3 * LANES)
    tokens = base.shape[0]
    whole = lambda shape: pl.BlockSpec(shape, lambda j: (0, 0), pipeline_mode=pl.Buffered(1))
    part = lambda rows, k: pl.BlockSpec((rows, LANES), lambda j, k=k: (0, k * count + j))
    return pl.pallas_call(
        ffn_kernel,
        grid=(count,),
        out_shape=jax.ShapeDtypeStruct(base.shape, dtype),
        in_specs=[
            pl.BlockSpec(memory_space=pltpu.SMEM),
            whole(x.shape),
            part(D, 0),
            part(D, 1),
            part(D, 2),
            part(16, 0),
            part(16, 1),
            whole(base.shape),
            whole(gate.shape),
        ],
        out_specs=pl.BlockSpec(base.shape, lambda j: (0, 0)),
        scratch_shapes=[pltpu.VMEM(base.shape, jnp.float32)],
        compiler_params=pltpu.CompilerParams(vmem_limit_bytes=58 << 20),
        cost_estimate=pl.CostEstimate(
            flops=2 * count * LANES * D * (2 * x.shape[0] + tokens),
            bytes_accessed=2 * weights.size + 8 * base.size,
            transcendentals=0,
        ),
    )(edges, x, weights, weights, weights, params, params, base, gate)


def local(
    n,
    hidden,
    keep_mask,
    kept_embed,
    time_mod,
    timestep,
    qkv_weight,
    proj_weight,
    norm_gain,
    in_weight,
    in_bias,
    conv_weight,
    conv_bias,
    out_weight,
):
    me = lax.axis_index("tile")
    f32 = jnp.float32
    steps = -(-FF // LANES)
    fill = ((0, 0), (0, steps * LANES - FF))
    shard = jnp.concatenate(
        [jnp.pad(piece, fill) for piece in (in_weight[:, :FF], in_weight[:, FF:], out_weight.T)],
        axis=1,
    )
    small = jnp.concatenate(
        [
            conv_weight.reshape(9, 2 * FF).astype(f32),
            conv_bias.astype(f32)[None],
            in_bias.astype(f32)[None],
            jnp.zeros((5, 2 * FF), f32),
        ],
        axis=0,
    )
    table = jnp.concatenate(
        [jnp.pad(small[:, :FF], fill), jnp.pad(small[:, FF:], fill)], axis=1
    )
    modulation = lax.dynamic_index_in_dim(time_mod, timestep[0], 0, keepdims=False).astype(f32)
    full, after_attn, framed = front(
        hidden,
        keep_mask.astype(f32)[:, None],
        kept_embed.astype(f32)[None],
        modulation,
        qkv_weight,
        proj_weight,
        norm_gain.astype(f32)[None],
        shard,
        n,
    )
    edges = jnp.stack([me > 0, me < n - 1]).astype(f32)
    weights = full.reshape(D, shard.shape[1])
    return ffn(framed, edges, weights, table, after_attn, modulation[5][None], jnp.bfloat16)


def solution(mesh):
    in_specs = (
        P(("groups", "tile"), None),
        P(("groups", "tile")),
        P(),
        P(),
        P("groups"),
        P(),
        P(),
        P(),
        P("tile", None),
        P(),
        P(),
        P(),
        P(None, "tile"),
    )
    return jax.shard_map(
        functools.partial(local, mesh.shape["tile"]),
        mesh=mesh,
        in_specs=in_specs,
        out_specs=P(("groups", "tile"), None),
        check_vma=False,
    )
```

time: 213 us -> 200 us (0.939)
  Pallas kernels: 23.8 us -> 189 us
  waiting for transfers between devices: 99.8 us -> 0 us
  matrix products: 39.8 us -> 0 us
  other arithmetic: 24.9 us -> 3.68 us
  between operations: 14.6 us -> 0.99 us
  starting transfers between devices: 4.37 us -> 0 us
    pallas_call x1 -> x2, Pallas kernels: 23.8 us -> 189 us  [the longest x1 143 us: front(): pl.pallas_call(functools.partial(front_kernel, n), out_shape=(jax.ShapeDt...]
    all_gather x2 -> x0, waiting for transfers between devices: 95.4 us -> none  [the longest x1 65.1 us: local(): in_full = lax.all_gather(in_weight, 'tile', axis=0, tiled=True)]
    dot_general x22 -> x0, matrix products: 39.8 us -> none  [the longest x1 17.6 us: local(): before = jnp.dot(framed, in_full, preferred_element_type=jnp.float32)]
    add x1 -> x0, other arithmetic: 10.5 us -> none  [convolve(): total + window[row_off:row_off + count, col_off:col_off + width, :].astyp...]
    convert_element_type x8 -> x2, other arithmetic: 5.62 us -> 0.62 us  [the longest x1 0.61 us: local(): edges = jnp.stack([me > 0, me < n - 1]).astype(f32)]
    ppermute x2 -> x0, starting transfers between devices: 4.33 us -> none  [the longest x1 2.86 us: local(): above = lax.ppermute(normed_ffn[tokens - CANVAS_W:], 'tile', down)]
    select_n x1 -> x0, other arithmetic: 3.79 us -> none  [local(): inner = jnp.where(inside, inner, jnp.zeros_like(inner))]
    ppermute x2 -> x0, waiting for transfers between devices: 3 us -> none  [the longest x1 3 us: local(): below = lax.ppermute(normed_ffn[:CANVAS_W], 'tile', up)]
  transfers between devices with their start and end apart: 4 -> 0, of which waited for: 3 -> 0; matrix products, arithmetic and copies ran while one was open for 28% -> 0% of each run, Pallas kernels for 11% -> 0%
where the time goes in v2:
time: 200 us; the launch traced here: 198 us
  Pallas kernels  189 us (94%)
  local copies, waits for them, and re-layouts  3.78 us (2%)
  other arithmetic  3.68 us (2%)
    pallas_call x1, Pallas kernels, front(): pl.pallas_call(functools.partial(front_kernel, n), out_shape=(jax.ShapeDt...  143 us
    pallas_call x1, Pallas kernels, ffn(): pl.pallas_call(ffn_kernel, grid=(count,), out_shape=jax.ShapeDtypeStruct(...  46.4 us

profile of v2, /device:TPU:0, one launch (start us, length us, event | category | flops | bytes accessed | tf_op | source)
XLA Modules:
  0.0 197.8 jit_solution(6675238149634959713)
XLA Ops:
  0.0 0.0 copy-start
  0.0 0.0 copy-start.9
  0.0 0.0 copy-start.7
  0.0 0.0 copy-start.8
  0.0 0.0 copy-start.2
  0.8 0.4 copy-done
  1.2 1.2 slice.21
  2.4 1.1 slice_select_fusion
  3.4 1.1 fusion.4.shard_ref
  4.5 0.0 copy-done.9
  4.6 0.1 broadcast_in_dim.42.mask_ref
  4.7 0.0 copy-done.7
  4.7 0.0 copy-done.8
  4.7 0.0 copy-done.2
  4.7 0.0 copy-start.3
  4.8 0.0 copy-start.4
  4.8 0.0 copy-start.5
  4.8 0.0 copy-start.6
  4.8 142.9 %shard_map.127 = (bf16[16,72,8832]{2,1,0:T(8,128)(2,1)}, f32[384,1152]{1,0:T(8,128)}, bf16[640,1152]{1,0:T(8,128)(2,1)S(1)}) custom-call(bf16[384,1152]{1,0:T(8,128)(2,1)S(1)} %copy-done.2, f32[384,1]{1,0:T(8,128)S(1)} %broadcast_in_dim.42.mask_ref, f32[1,1152]{1,0:T(1,128)S(1)} %reshape.9.embed_ref, f32[6,1152]{1,0:T(8,128)S(1)} %get-tuple-element.12.mod_ref, ...), custom_call_target="tpu_custom_call" | custom-call | tf_op jit(solution)/shard_map/pallas_call | solution.py:397
  147.7 0.0 copy-start.1
  147.8 1.2 copy-done.1
  148.9 0.6 slice_bitcast_fusion.gate_ref
  149.5 0.0 copy-done.3
  149.5 0.1 reshape.11
  149.6 0.0 copy-done.4
  149.6 0.0 copy-done.5
  149.7 0.1 pad.27.clone
  149.7 0.1 maximum_maximum_fusion
  149.8 0.1 slice.27
  150.0 0.0 copy-done.6
  150.0 0.8 select_maximum_fusion.pa_ref.pb_ref
  150.8 0.6 add_convert_fusion.edge_ref
  151.4 46.4 %shard_map.128 = bf16[384,1152]{1,0:T(8,128)(2,1)} custom-call(f32[2]{0:T(128)} %add_convert_fusion.edge_ref, bf16[640,1152]{1,0:T(8,128)(2,1)} %copy-done.1, bf16[1152,8832]{1,0:T(8,128)(2,1)} %bitcast.12, bf16[1152,8832]{1,0:T(8,128)(2,1)} %bitcast.13, bf16[1152,8832]{1,0:T(8,128)(2,1)} %bitcast.14, f32[16,5888]{1,0:T(8,128)} %select_maximum_fusion.pa_ref.pb_ref, ...), custom_call_target="tpu_custom_call" | custom-call | flops 11286872064 | bytes 23887872 | tf_op jit(solution)/shard_map/pallas_call | solution.py:511
  (9 shorter events, 0.1 us)
Async XLA Ops:
  0.0 1.1 copy-start
  0.0 4.5 %copy-start.9 = (s32[384]{0:T(512)S(1)}, s32[384]{0:T(512)}, u32[]{:S(2)}) copy-start(s32[384]{0:T(512)} %param.14) | copy-start | bytes 4612
  0.0 4.7 %copy-start.7 = (bf16[1152]{0:T(1024)(128)(2,1)S(1)}, bf16[1152]{0:T(1024)(128)(2,1)}, u32[]{:S(2)}) copy-start(bf16[1152]{0:T(1024)(128)(2,1)} %param.20) | copy-start | bytes 6916
  0.0 4.7 %copy-start.8 = (bf16[1152]{0:T(1024)(128)(2,1)S(1)}, bf16[1152]{0:T(1024)(128)(2,1)}, u32[]{:S(2)}) copy-start(bf16[1152]{0:T(1024)(128)(2,1)} %param.15) | copy-start | bytes 6916
  0.0 4.7 %copy-start.2 = (bf16[384,1152]{1,0:T(8,128)(2,1)S(1)}, bf16[384,1152]{1,0:T(8,128)(2,1)}, u32[]{:S(2)}) copy-start(bf16[384,1152]{1,0:T(8,128)(2,1)} %hidden_ref.1) | copy-start | bytes 2654212
  4.7 144.8 %copy-start.3 = (bf16[3,3,5760]{2,1,0:T(4,128)(2,1)S(1)}, bf16[3,3,5760]{2,1,0:T(4,128)(2,1)}, u32[]{:S(2)}) copy-start(bf16[3,3,5760]{2,1,0:T(4,128)(2,1)} %param.23) | copy-start | bytes 311044
  4.8 144.8 %copy-start.4 = (bf16[5760]{0:T(1024)(128)(2,1)S(1)}, bf16[5760]{0:T(1024)(128)(2,1)}, u32[]{:S(2)}) copy-start(bf16[5760]{0:T(1024)(128)(2,1)} %param.24) | copy-start | bytes 34564
  4.8 144.9 %copy-start.5 = (bf16[5760]{0:T(1024)(128)(2,1)S(1)}, bf16[5760]{0:T(1024)(128)(2,1)}, u32[]{:S(2)}) copy-start(bf16[5760]{0:T(1024)(128)(2,1)} %param.22) | copy-start | bytes 34564
  4.8 145.2 %copy-start.6 = (pred[2944]{0:T(1024)(128)(4,1)S(1)}, pred[2944]{0:T(1024)(128)(4,1)}, u32[]{:S(2)}) copy-start(pred[2944]{0:T(1024)(128)(4,1)} %constant.18.clone.1) | copy-start | bytes 8836
  147.7 1.2 copy-start.1

commit v3 on v2

--- a/solution.py
+++ b/solution.py
@@ -23,6 +23,12 @@
     while (2 * wide) ** 2 <= n // 2:
         wide *= 2
     return n // (2 * wide), wide
+
+
+def unit_rows(rows):
+    units = 4 if rows >= 32 else 2
+    marks = [min(-(-rows * u // (8 * units)) * 8, rows) for u in range(units + 1)]
+    return [slice(lo, hi) for lo, hi in zip(marks[:-1], marks[1:])]
 
 
 def front_kernel(
@@ -65,8 +71,8 @@
     at_b = lax.rem(me // 2, count_b)
     at_a = me // (2 * count_b)
     rows = shard_ref.shape[0]
-    cut = -(-rows // 16) * 8
-    rows_of = (slice(0, cut), slice(cut, rows))
+    rows_of = unit_rows(rows)
+    units = len(rows_of)
     per = mine.shape[0]
     tokens = hidden_ref.shape[0]
 
@@ -118,7 +124,7 @@
             a,
             at_b,
             p,
-            side_send.at[k, a],
+            side_send.at[k, a, p],
             arrive,
             {"tile": tile_of(at_a, lax.rem(at_b + k, count_b), core)},
         )
@@ -129,7 +135,7 @@
             a,
             b,
             p,
-            group_send.at[a, b],
+            group_send.at[a, b, p],
             arrive,
             {"groups": 1 - plane},
         )
@@ -157,20 +163,91 @@
         ).wait_recv()
 
     ways = ((at_a < count_a - 1), (at_a > 0))
+
+    def onward(d, p, way):
+        if d < count_a - 2:
+            return ways[way]
+        return jnp.logical_and(ways[way], plane == p % 2)
     keep = pltpu.make_async_copy(shard_ref, full_ref.at[me], own_sem)
     keep.start()
-    for p in range(2):
+    for p in range(units):
         for way in range(2):
-            @pl.when(ways[way])
+            @pl.when(onward(0, p, way))
             def _():
                 line(at_a, p, way, True).start()
 
-        @pl.when(plane == p)
+        @pl.when(plane == p % 2)
         def _():
             for k in range(1, count_b):
                 side(at_a, k, p, True).start()
 
         twin(at_a, at_b, p, True).start()
+
+    def near(d):
+        if d == 0:
+            return [(at_a, None, 0)]
+        if not 0 < d < count_a:
+            return []
+        return [(at_a - d, at_a >= d, 0), (at_a + d, at_a < count_a - d, 1)]
+
+    def under(cond, do):
+        if cond is None:
+            do()
+        else:
+            pl.when(cond)(do)
+
+    def forward(stage):
+        for a, ok, way in near(stage):
+            def from_line(a=a, way=way):
+                for p in range(units):
+                    def one(p=p):
+                        arrived(a, at_b, p)
+                        if stage < count_a - 1:
+                            @pl.when(onward(stage, p, way))
+                            def _():
+                                line(a, p, way).start()
+
+                        @pl.when(plane == p % 2)
+                        def _():
+                            for k in range(1, count_b):
+                                side(a, k, p).start()
+                            if stage == count_a - 1:
+                                group(a, at_b, p).start()
+
+                        twin(a, at_b, p).start()
+
+                    under((plane == p % 2) if stage == count_a - 1 else None, one)
+
+            under(ok, from_line)
+        for a, ok, way in near(stage - 1):
+            def from_side(a=a):
+                for p in range(units):
+                    if stage - 1 == count_a - 1:
+                        @pl.when(plane != p % 2)
+                        def _():
+                            arrived(a, at_b, p)
+                            twin(a, at_b, p).start()
+
+                    @pl.when(plane == p % 2)
+                    def _():
+                        for k in range(1, count_b):
+                            b = lax.rem(at_b + k, count_b)
+                            arrived(a, b, p)
+                            group(a, b, p).start()
+                            twin(a, b, p).start()
+
+            under(ok, from_side)
+        for a, ok, way in near(stage - 2):
+            def from_group(a=a):
+                for p in range(units):
+                    @pl.when(plane != p % 2)
+                    def _():
+                        for k in range(1, count_b):
+                            b = lax.rem(at_b + k, count_b)
+                            arrived(a, b, p)
+                            twin(a, b, p).start()
+
+            under(ok, from_group)
 
     stream = hidden_ref[...].astype(jnp.float32) + mask_ref[...] * embed_ref[...]
     normed[...] = modulated_norm(stream, mod_ref[0:1, :], mod_ref[1:2, :]).astype(jnp.bfloat16)
@@ -239,6 +316,7 @@
         lax.fori_loop(1, n, body, 0)
 
     each(lambda k: scatter(k).start())
+    forward(1)
     mine[...] = part[pl.ds(pl.multiple_of(me * per, 8), per), :]
 
     def gather(k):
@@ -304,58 +382,8 @@
     def _():
         frame_ref[CANVAS_W + tokens :, :] = jnp.zeros((CANVAS_W, D), jnp.bfloat16)
 
-    def near(d):
-        if d == 0:
-            return [(at_a, None, 0)]
-        return [(at_a - d, at_a >= d, 0), (at_a + d, at_a < count_a - d, 1)]
-
-    def under(cond, do):
-        if cond is None:
-            do()
-        else:
-            pl.when(cond)(do)
-
-    for stage in range(1, count_a + 2):
-        for a, ok, way in near(stage) if stage < count_a else []:
-            def from_line(a=a, way=way):
-                for p in range(2):
-                    arrived(a, at_b, p)
-
-                    @pl.when(ways[way])
-                    def _():
-                        line(a, p, way).start()
-
-                    @pl.when(plane == p)
-                    def _():
-                        for k in range(1, count_b):
-                            side(a, k, p).start()
-
-                    twin(a, at_b, p).start()
-
-            under(ok, from_line)
-        for a, ok, way in near(stage - 1) if stage - 1 < count_a else []:
-            def from_side(a=a):
-                for k in range(1, count_b):
-                    b = lax.rem(at_b + k, count_b)
-                    for p in range(2):
-                        @pl.when(plane == p)
-                        def _():
-                            arrived(a, b, p)
-                            group(a, b, p).start()
-                            twin(a, b, p).start()
-
-            under(ok, from_side)
-        for a, ok, way in near(stage - 2) if 0 <= stage - 2 < count_a else []:
-            def from_group(a=a):
-                for k in range(1, count_b):
-                    b = lax.rem(at_b + k, count_b)
-                    for p in range(2):
-                        @pl.when(plane != p)
-                        def _():
-                            arrived(a, b, p)
-                            twin(a, b, p).start()
-
-            under(ok, from_group)
+    for stage in range(2, count_a + 2):
+        forward(stage)
 
     keep.wait()
     for way in range(2):
@@ -368,21 +396,27 @@
             halo(way).wait_recv()
 
     for a in range(count_a):
-        for p in range(2):
-            @pl.when(jnp.logical_and(ways[0], at_a >= a))
-            def _():
-                line(a, p, 0).wait_send()
-
-            @pl.when(jnp.logical_and(ways[1], at_a <= a))
-            def _():
-                line(a, p, 1).wait_send()
-
-            @pl.when(plane == p)
+        far = (at_a - a == count_a - 1, a - at_a == count_a - 1)
+        for p in range(units):
+            for way in range(2):
+                reach = (at_a >= a, at_a <= a)[way]
+                last = (at_a - a == count_a - 2, a - at_a == count_a - 2)[way]
+                sent = jnp.logical_or(jnp.logical_not(last), plane == p % 2)
+
+                @pl.when(jnp.logical_and(jnp.logical_and(ways[way], reach), sent))
+                def _():
+                    line(a, p, way).wait_send()
+
+            @pl.when(plane == p % 2)
             def _():
                 for k in range(1, count_b):
                     side(a, k, p).wait_send()
                     group(a, lax.rem(at_b + k, count_b), p).wait_send()
 
+                @pl.when(jnp.logical_or(far[0], far[1]))
+                def _():
+                    group(a, at_b, p).wait_send()
+
             for b in range(count_b):
                 twin(a, b, p).wait_send()
                 arrived(a, b, p, sibling, 1 - core)
@@ -390,6 +424,7 @@
 
 def front(hidden, mask, embed, mod, qkv_weight, proj_weight, gain, shard, n):
     count_a, count_b = mesh_box(n)
+    units = len(unit_rows(shard.shape[0]))
     tokens = hidden.shape[0]
     per = -(-GROUPS * HEAD_DIM // (8 * n)) * 8
     vmem = pl.BlockSpec(memory_space=pltpu.VMEM)
@@ -416,12 +451,12 @@
             dma((n,)),
             dma((2,)),
             dma((2,)),
-            dma((2, count_a, 2)),
-            dma((count_b, count_a)),
-            dma((count_a, count_b)),
-            dma((count_a, count_b, 2)),
-            dma((count_a, count_b, 2)),
-            dma((count_a, count_b, 2)),
+            dma((2, count_a, units)),
+            dma((count_b, count_a, units)),
+            dma((count_a, count_b, units)),
+            dma((count_a, count_b, units)),
+            dma((count_a, count_b, units)),
+            dma((count_a, count_b, units)),
             dma,
         ],
         compiler_params=pltpu.CompilerParams(

time: 200 us -> 200 us (level)
  no operation moved by 1% of the time
where the time goes in v3:
time: 200 us; the launch traced here: 197 us
  Pallas kernels  189 us (94%)
  local copies, waits for them, and re-layouts  3.78 us (2%)
  other arithmetic  3.68 us (2%)
    pallas_call x1, Pallas kernels, front(): pl.pallas_call(functools.partial(front_kernel, n), out_shape=(jax.ShapeDt...  142 us
    pallas_call x1, Pallas kernels, ffn(): pl.pallas_call(ffn_kernel, grid=(count,), out_shape=jax.ShapeDtypeStruct(...  46.4 us

profile of v3, /device:TPU:0, one launch (start us, length us, event | category | flops | bytes accessed | tf_op | source)
XLA Modules:
  0.0 197.2 jit_solution(16181669262426402940)
XLA Ops:
  0.0 0.0 copy-start
  0.0 0.0 copy-start.9
  0.0 0.0 copy-start.7
  0.0 0.0 copy-start.8
  0.0 0.0 copy-start.2
  0.8 0.4 copy-done
  1.2 1.2 slice.21
  2.4 1.1 slice_select_fusion
  3.4 1.1 fusion.4.shard_ref
  4.5 0.0 copy-done.9
  4.6 0.1 broadcast_in_dim.42.mask_ref
  4.7 0.0 copy-done.7
  4.7 0.0 copy-done.8
  4.7 0.0 copy-done.2
  4.7 0.0 copy-start.3
  4.8 0.0 copy-start.4
  4.8 0.0 copy-start.5
  4.8 0.0 copy-start.6
  4.8 142.4 %shard_map.127 = (bf16[16,72,8832]{2,1,0:T(8,128)(2,1)}, f32[384,1152]{1,0:T(8,128)}, bf16[640,1152]{1,0:T(8,128)(2,1)S(1)}) custom-call(bf16[384,1152]{1,0:T(8,128)(2,1)S(1)} %copy-done.2, f32[384,1]{1,0:T(8,128)S(1)} %broadcast_in_dim.42.mask_ref, f32[1,1152]{1,0:T(1,128)S(1)} %reshape.9.embed_ref, f32[6,1152]{1,0:T(8,128)S(1)} %get-tuple-element.12.mod_ref, ...), custom_call_target="tpu_custom_call" | custom-call | tf_op jit(solution)/shard_map/pallas_call | solution.py:432
  147.2 0.0 copy-start.1
  147.2 1.2 copy-done.1
  148.4 0.6 slice_bitcast_fusion.gate_ref
  149.0 0.0 copy-done.3
  149.0 0.1 reshape.11
  149.1 0.0 copy-done.4
  149.1 0.0 copy-done.5
  149.1 0.1 pad.27.clone
  149.2 0.1 maximum_maximum_fusion
  149.3 0.1 slice.27
  149.4 0.0 copy-done.6
  149.5 0.8 select_maximum_fusion.pa_ref.pb_ref
  150.3 0.6 add_convert_fusion.edge_ref
  150.9 46.4 %shard_map.128 = bf16[384,1152]{1,0:T(8,128)(2,1)} custom-call(f32[2]{0:T(128)} %add_convert_fusion.edge_ref, bf16[640,1152]{1,0:T(8,128)(2,1)} %copy-done.1, bf16[1152,8832]{1,0:T(8,128)(2,1)} %bitcast.12, bf16[1152,8832]{1,0:T(8,128)(2,1)} %bitcast.13, bf16[1152,8832]{1,0:T(8,128)(2,1)} %bitcast.14, f32[16,5888]{1,0:T(8,128)} %select_maximum_fusion.pa_ref.pb_ref, ...), custom_call_target="tpu_custom_call" | custom-call | flops 11286872064 | bytes 23887872 | tf_op jit(solution)/shard_map/pallas_call | solution.py:546
  (9 shorter events, 0.1 us)
Async XLA Ops:
  0.0 1.1 copy-start
  0.0 4.5 %copy-start.9 = (s32[384]{0:T(512)S(1)}, s32[384]{0:T(512)}, u32[]{:S(2)}) copy-start(s32[384]{0:T(512)} %param.14) | copy-start | bytes 4612
  0.0 4.7 %copy-start.7 = (bf16[1152]{0:T(1024)(128)(2,1)S(1)}, bf16[1152]{0:T(1024)(128)(2,1)}, u32[]{:S(2)}) copy-start(bf16[1152]{0:T(1024)(128)(2,1)} %param.20) | copy-start | bytes 6916
  0.0 4.7 %copy-start.8 = (bf16[1152]{0:T(1024)(128)(2,1)S(1)}, bf16[1152]{0:T(1024)(128)(2,1)}, u32[]{:S(2)}) copy-start(bf16[1152]{0:T(1024)(128)(2,1)} %param.15) | copy-start | bytes 6916
  0.0 4.7 %copy-start.2 = (bf16[384,1152]{1,0:T(8,128)(2,1)S(1)}, bf16[384,1152]{1,0:T(8,128)(2,1)}, u32[]{:S(2)}) copy-start(bf16[384,1152]{1,0:T(8,128)(2,1)} %hidden_ref.1) | copy-start | bytes 2654212
  4.7 144.2 %copy-start.3 = (bf16[3,3,5760]{2,1,0:T(4,128)(2,1)S(1)}, bf16[3,3,5760]{2,1,0:T(4,128)(2,1)}, u32[]{:S(2)}) copy-start(bf16[3,3,5760]{2,1,0:T(4,128)(2,1)} %param.23) | copy-start | bytes 311044
  4.8 144.3 %copy-start.4 = (bf16[5760]{0:T(1024)(128)(2,1)S(1)}, bf16[5760]{0:T(1024)(128)(2,1)}, u32[]{:S(2)}) copy-start(bf16[5760]{0:T(1024)(128)(2,1)} %param.24) | copy-start | bytes 34564
  4.8 144.3 %copy-start.5 = (bf16[5760]{0:T(1024)(128)(2,1)S(1)}, bf16[5760]{0:T(1024)(128)(2,1)}, u32[]{:S(2)}) copy-start(bf16[5760]{0:T(1024)(128)(2,1)} %param.22) | copy-start | bytes 34564
  4.8 144.7 %copy-start.6 = (pred[2944]{0:T(1024)(128)(4,1)S(1)}, pred[2944]{0:T(1024)(128)(4,1)}, u32[]{:S(2)}) copy-start(pred[2944]{0:T(1024)(128)(4,1)} %constant.18.clone.1) | copy-start | bytes 8836
  147.2 1.2 copy-start.1

commit v4 on v3

--- a/solution.py
+++ b/solution.py
@@ -496,9 +496,11 @@
     not_left = column > 0
     not_right = column < CANVAS_W - 1
 
-    def filtered(w_ref, p_ref):
-        v = jnp.dot(x, w_ref[...], preferred_element_type=jnp.float32) + p_ref[10:11, :]
-        e = silu(v).astype(jnp.bfloat16).astype(jnp.float32)
+    both = jnp.concatenate([wa_ref[...], wb_ref[...]], axis=1)
+    wide = jnp.dot(x, both, preferred_element_type=jnp.float32)
+
+    def filtered(v, p_ref):
+        e = silu(v + p_ref[10:11, :]).astype(jnp.bfloat16).astype(jnp.float32)
         lines = [e[r * CANVAS_W : (r + 1) * CANVAS_W] for r in range(frame // CANVAS_W)]
         lines[0] = lines[0] * edge_ref[0]
         lines[-1] = lines[-1] * edge_ref[1]
@@ -516,8 +518,8 @@
             out.append(left + side[1] + right + p_ref[9:10, :])
         return out
 
-    first_half = filtered(wa_ref, pa_ref)
-    second_half = filtered(wb_ref, pb_ref)
+    first_half = filtered(wide[:, :LANES], pa_ref)
+    second_half = filtered(wide[:, LANES:], pb_ref)
     gated = jnp.concatenate(
         [(a * silu(b)).astype(jnp.bfloat16) for a, b in zip(first_half, second_half)], axis=0
     )

time: 200 us -> 202 us (1.010)
    pallas_call x1, Pallas kernels: 46.4 us -> 48.6 us  [ffn(): pl.pallas_call(ffn_kernel, grid=(count,), out_shape=jax.ShapeDtypeStruct(...]
where the time goes in v4:
time: 202 us; the launch traced here: 199 us
  Pallas kernels  191 us (95%)
  local copies, waits for them, and re-layouts  3.78 us (2%)
  other arithmetic  3.68 us (2%)
    pallas_call x1, Pallas kernels, front(): pl.pallas_call(functools.partial(front_kernel, n), out_shape=(jax.ShapeDt...  142 us
    pallas_call x1, Pallas kernels, ffn(): pl.pallas_call(ffn_kernel, grid=(count,), out_shape=jax.ShapeDtypeStruct(...  48.6 us

profile of v4, /device:TPU:0, one launch (start us, length us, event | category | flops | bytes accessed | tf_op | source)
XLA Modules:
  0.0 199.5 jit_solution(3225323551569928900)
XLA Ops:
  0.0 0.0 copy-start
  0.0 0.0 copy-start.9
  0.0 0.0 copy-start.7
  0.0 0.0 copy-start.8
  0.0 0.0 copy-start.2
  0.8 0.4 copy-done
  1.2 1.2 slice.21
  2.4 1.1 slice_select_fusion
  3.4 1.1 fusion.4.shard_ref
  4.5 0.0 copy-done.9
  4.6 0.1 broadcast_in_dim.42.mask_ref
  4.7 0.0 copy-done.7
  4.7 0.0 copy-done.8
  4.7 0.0 copy-done.2
  4.7 0.0 copy-start.3
  4.8 0.0 copy-start.4
  4.8 0.0 copy-start.5
  4.8 0.0 copy-start.6
  4.8 142.4 %shard_map.127 = (bf16[16,72,8832]{2,1,0:T(8,128)(2,1)}, f32[384,1152]{1,0:T(8,128)}, bf16[640,1152]{1,0:T(8,128)(2,1)S(1)}) custom-call(bf16[384,1152]{1,0:T(8,128)(2,1)S(1)} %copy-done.2, f32[384,1]{1,0:T(8,128)S(1)} %broadcast_in_dim.42.mask_ref, f32[1,1152]{1,0:T(1,128)S(1)} %reshape.9.embed_ref, f32[6,1152]{1,0:T(8,128)S(1)} %get-tuple-element.12.mod_ref, ...), custom_call_target="tpu_custom_call" | custom-call | tf_op jit(solution)/shard_map/pallas_call | solution.py:432
  147.2 0.0 copy-start.1
  147.2 1.2 copy-done.1
  148.4 0.6 slice_bitcast_fusion.gate_ref
  149.0 0.0 copy-done.3
  149.0 0.1 reshape.11
  149.1 0.0 copy-done.4
  149.1 0.0 copy-done.5
  149.1 0.1 pad.27.clone
  149.2 0.1 maximum_maximum_fusion
  149.3 0.1 slice.27
  149.4 0.0 copy-done.6
  149.5 0.8 select_maximum_fusion.pa_ref.pb_ref
  150.3 0.6 add_convert_fusion.edge_ref
  150.9 48.6 %shard_map.128 = bf16[384,1152]{1,0:T(8,128)(2,1)} custom-call(f32[2]{0:T(128)} %add_convert_fusion.edge_ref, bf16[640,1152]{1,0:T(8,128)(2,1)} %copy-done.1, bf16[1152,8832]{1,0:T(8,128)(2,1)} %bitcast.12, bf16[1152,8832]{1,0:T(8,128)(2,1)} %bitcast.13, bf16[1152,8832]{1,0:T(8,128)(2,1)} %bitcast.14, f32[16,5888]{1,0:T(8,128)} %select_maximum_fusion.pa_ref.pb_ref, ...), custom_call_target="tpu_custom_call" | custom-call | flops 11286872064 | bytes 23887872 | tf_op jit(solution)/shard_map/pallas_call | solution.py:548
  (9 shorter events, 0.1 us)
Async XLA Ops:
  0.0 1.1 copy-start
  0.0 4.5 %copy-start.9 = (s32[384]{0:T(512)S(1)}, s32[384]{0:T(512)}, u32[]{:S(2)}) copy-start(s32[384]{0:T(512)} %param.14) | copy-start | bytes 4612
  0.0 4.7 %copy-start.7 = (bf16[1152]{0:T(1024)(128)(2,1)S(1)}, bf16[1152]{0:T(1024)(128)(2,1)}, u32[]{:S(2)}) copy-start(bf16[1152]{0:T(1024)(128)(2,1)} %param.20) | copy-start | bytes 6916
  0.0 4.7 %copy-start.8 = (bf16[1152]{0:T(1024)(128)(2,1)S(1)}, bf16[1152]{0:T(1024)(128)(2,1)}, u32[]{:S(2)}) copy-start(bf16[1152]{0:T(1024)(128)(2,1)} %param.15) | copy-start | bytes 6916
  0.0 4.7 %copy-start.2 = (bf16[384,1152]{1,0:T(8,128)(2,1)S(1)}, bf16[384,1152]{1,0:T(8,128)(2,1)}, u32[]{:S(2)}) copy-start(bf16[384,1152]{1,0:T(8,128)(2,1)} %hidden_ref.1) | copy-start | bytes 2654212
  4.7 144.2 %copy-start.3 = (bf16[3,3,5760]{2,1,0:T(4,128)(2,1)S(1)}, bf16[3,3,5760]{2,1,0:T(4,128)(2,1)}, u32[]{:S(2)}) copy-start(bf16[3,3,5760]{2,1,0:T(4,128)(2,1)} %param.23) | copy-start | bytes 311044
  4.8 144.3 %copy-start.4 = (bf16[5760]{0:T(1024)(128)(2,1)S(1)}, bf16[5760]{0:T(1024)(128)(2,1)}, u32[]{:S(2)}) copy-start(bf16[5760]{0:T(1024)(128)(2,1)} %param.24) | copy-start | bytes 34564
  4.8 144.3 %copy-start.5 = (bf16[5760]{0:T(1024)(128)(2,1)S(1)}, bf16[5760]{0:T(1024)(128)(2,1)}, u32[]{:S(2)}) copy-start(bf16[5760]{0:T(1024)(128)(2,1)} %param.22) | copy-start | bytes 34564
  4.8 144.7 %copy-start.6 = (pred[2944]{0:T(1024)(128)(4,1)S(1)}, pred[2944]{0:T(1024)(128)(4,1)}, u32[]{:S(2)}) copy-start(pred[2944]{0:T(1024)(128)(4,1)} %constant.18.clone.1) | copy-start | bytes 8836
  147.2 1.2 copy-start.1
